TPU v7x, 32 devices: a whole 2x2x4 slice. The times are simulated.
32 devices in a mesh: slab: 8 (over y, x, core), blk: 4 (over z).
Axes of the slice: x: 2, y: 2, z: 4, core: 2. Of those that a mesh axis runs over, the one named last changes fastest.
Arguments:
- start_block: float32 [128, 64, 8, 128], P('blk', 'slab'), as said below
- locked_modes: float32 [384, 64, 8, 128], P('blk', 'slab'), as said below
- material: int32 [64, 8, 128], P('slab'), may hold values 0 or 1
- support: int32 [8, 128], replicated, may hold values 0 or 1
Outputs:
- basis: float32 [128, 64, 8, 128], P('blk', 'slab')
Inputs may be any that keep to these rules, and one draw needn't show every extreme that they name: `start_block`: A block of random vectors with large parts along the locked modes. `locked_modes`: each locked mode (one row) has about unit norm over all voxels.
All inputs are finite; a program needn't handle non-finite values. No bound on the sum of `material` on one device may be relied on, other than what follows from the above.
Results may differ from a plain program's by a relative error of at most 0.00014.
Values sent between devices are 32-bit elements; how exact they have to be, the bound alone decides.
No kernel may reach another device: no remote copies, remote signals or barrier semaphores. Data moves between devices by JAX's collectives and lax.ppermute only.
A program may use at most 64 MiB of HBM per device.

v0:
```python
import jax
import jax.numpy as jnp
from jax import lax
from jax.sharding import PartitionSpec as P

DEGREE = 8
THETA_LOAD = 0.1
VOID_ROOT = 0.31622776601683794
FILTER_CENTRE = 9.0
FILTER_HALF = 7.5


def padded_2(cells, sides, width):
    for axis, dim in sides:
        count = lax.axis_size(axis)
        ends = count - 1
        head = lax.slice_in_dim(cells, 0, width, axis=dim)
        tail = lax.slice_in_dim(cells, cells.shape[dim] - width, cells.shape[dim], axis=dim)
        cells = jnp.concatenate(
            [
                lax.ppermute(tail, axis, [(i, (i + 1) % count) for i in range(ends)]),
                cells,
                lax.ppermute(head, axis, [((i + 1) % count, i) for i in range(ends)]),
            ],
            axis=dim,
        )
    return cells


def blurred(padded):
    along_z = 0.5 * padded[:, :-2] + padded[:, 1:-1] + 0.5 * padded[:, 2:]
    along_y = 0.5 * along_z[:, :, :-2] + along_z[:, :, 1:-1] + 0.5 * along_z[:, :, 2:]
    along_x = 0.5 * along_y[..., :-2] + along_y[..., 1:-1] + 0.5 * along_y[..., 2:]
    return 2.0 * along_x


def operate(field, free_cells, root_stiff):
    kept_field = free_cells * field
    weighted = root_stiff * kept_field
    extended = padded_2(weighted, (("slab", 1),), 1)
    padded = jnp.pad(extended, ((0, 0), (0, 0), (1, 1), (1, 1)))
    smooth = blurred(padded)
    neighbours = padded[:, 2:, 1:-1, 1:-1] + padded[:, :-2, 1:-1, 1:-1]
    elastic = root_stiff * (16.0 * weighted - smooth)
    geometric = THETA_LOAD * root_stiff * (2.0 * weighted - neighbours)
    return free_cells * (elastic - geometric + 0.5 * kept_field) + (1.0 - free_cells) * field


def lower_inverse(gram):
    lower_factor = jnp.linalg.cholesky(gram)
    identity = jnp.eye(gram.shape[0], dtype=jnp.float32)
    return jax.scipy.linalg.solve_triangular(lower_factor, identity, lower=True)


def per_device(start_block, locked_modes, material, support):
    depth = material.shape[0]
    root_stiff = jnp.where(material == 1, 1.0, VOID_ROOT).astype(jnp.float32)
    layer = lax.axis_index("slab") * depth + lax.broadcasted_iota(jnp.int32, material.shape, 0)
    clamped = jnp.where(layer == 0, support[None, :, :], 0)
    free_cells = (1 - clamped).astype(jnp.float32)
    previous = start_block
    current = (
        operate(start_block, free_cells, root_stiff) - FILTER_CENTRE * start_block
    ) / FILTER_HALF
    for order_index in range(DEGREE - 1):
        following = (
            2.0 * (operate(current, free_cells, root_stiff) - FILTER_CENTRE * current) / FILTER_HALF
            - previous
        )
        previous = current
        current = following
    own_count = start_block.shape[0]
    cells = depth * start_block.shape[2] * start_block.shape[3]
    total_cells = cells * lax.axis_size("slab")
    flat = current.reshape(own_count, cells)
    modes_flat = locked_modes.reshape(locked_modes.shape[0], cells)
    gathered = lax.all_gather(flat, "blk", axis=0, tiled=True)
    correlations = lax.psum(
        jnp.dot(
            modes_flat,
            gathered.T,
            precision=lax.Precision.HIGHEST,
            preferred_element_type=jnp.float32,
        ),
        "slab",
    )
    own_deflated = flat - lax.psum_scatter(
        jnp.dot(
            correlations.T,
            modes_flat,
            precision=lax.Precision.HIGHEST,
            preferred_element_type=jnp.float32,
        ),
        "blk",
        scatter_dimension=0,
        tiled=True,
    )
    deflated = lax.all_gather(own_deflated, "blk", axis=0, tiled=True)
    gram = lax.psum(
        jnp.dot(
            deflated,
            deflated.T,
            precision=lax.Precision.HIGHEST,
            preferred_element_type=jnp.float32,
        ),
        "slab",
    )
    inverse = lower_inverse(gram)
    own_rows = lax.dynamic_slice_in_dim(inverse, lax.axis_index("blk") * own_count, own_count, 0)
    basis = jnp.sqrt(jnp.float32(total_cells)) * jnp.dot(
        own_rows, deflated, precision=lax.Precision.HIGHEST, preferred_element_type=jnp.float32
    )
    return basis.reshape(start_block.shape)


def solution(mesh):
    in_specs = (
        P("blk", "slab", None, None),
        P("blk", "slab", None, None),
        P("slab", None, None),
        P(),
    )
    out_specs = P("blk", "slab", None, None)
    return jax.shard_map(
        per_device, mesh=mesh, in_specs=in_specs, out_specs=out_specs, check_vma=False
    )
```

profile of v0, /device:TPU:0, one launch (start us, length us, event | category | flops | bytes accessed | tf_op | source)
XLA Modules:
  0.0 502.9 jit_solution(1023885015626496293)
XLA Ops:
  8.1 1.3 multiply_multiply_fusion.7
  9.5 1.3 collective-permute-start.1
  10.8 3.0 collective-permute-start
  14.8 2.2 select_maximum_fusion.14
  21.6 6.1 %collective-permute-start.2 = (f32[32,1,8,128]{3,2,1,0:T(8,128)S(1)}, f32[32,1,8,128]{3,2,1,0:T(8,128)S(1)}, u32[]{:S(2)}, u32[]{:S(2)}) collective-permute-start(f32[32,1,8,128]{3,2,1,0:T(8,128)S(1)} %get-tuple-element.32), channel_id=1, source_target_pairs={{0,4},{4,8},{8,12},{12,16},{16,20},{20,24},{24,28},{1,5},{5,9},{9,... | collective-permute-start | bytes 393224 | tf_op jit(solution)/shard_map/ppermute | solution.py:21
  28.7 2.2 select_maximum_fusion.12
  34.9 6.1 %collective-permute-start.4 = (f32[32,1,8,128]{3,2,1,0:T(8,128)S(1)}, f32[32,1,8,128]{3,2,1,0:T(8,128)S(1)}, u32[]{:S(2)}, u32[]{:S(2)}) collective-permute-start(f32[32,1,8,128]{3,2,1,0:T(8,128)S(1)} %get-tuple-element.30), channel_id=1, source_target_pairs={{0,4},{4,8},{8,12},{12,16},{16,20},{20,24},{24,28},{1,5},{5,9},{9,... | collective-permute-start | bytes 393224 | tf_op jit(solution)/shard_map/ppermute | solution.py:21
  41.8 2.2 select_maximum_fusion.10
  48.1 5.9 %collective-permute-start.6 = (f32[32,1,8,128]{3,2,1,0:T(8,128)S(1)}, f32[32,1,8,128]{3,2,1,0:T(8,128)S(1)}, u32[]{:S(2)}, u32[]{:S(2)}) collective-permute-start(f32[32,1,8,128]{3,2,1,0:T(8,128)S(1)} %get-tuple-element.28), channel_id=1, source_target_pairs={{0,4},{4,8},{8,12},{12,16},{16,20},{20,24},{24,28},{1,5},{5,9},{9,... | collective-permute-start | bytes 393224 | tf_op jit(solution)/shard_map/ppermute | solution.py:21
  55.0 2.2 select_maximum_fusion.8
  60.0 1.3 collective-permute-start.9
  61.3 5.9 %collective-permute-start.8 = (f32[32,1,8,128]{3,2,1,0:T(8,128)S(1)}, f32[32,1,8,128]{3,2,1,0:T(8,128)S(1)}, u32[]{:S(2)}, u32[]{:S(2)}) collective-permute-start(f32[32,1,8,128]{3,2,1,0:T(8,128)S(1)} %get-tuple-element.26), channel_id=1, source_target_pairs={{0,4},{4,8},{8,12},{12,16},{16,20},{20,24},{24,28},{1,5},{5,9},{9,... | collective-permute-start | bytes 393224 | tf_op jit(solution)/shard_map/ppermute | solution.py:21
  68.2 2.2 select_maximum_fusion.6
  74.4 6.2 %collective-permute-start.10 = (f32[32,1,8,128]{3,2,1,0:T(8,128)S(1)}, f32[32,1,8,128]{3,2,1,0:T(8,128)S(1)}, u32[]{:S(2)}, u32[]{:S(2)}) collective-permute-start(f32[32,1,8,128]{3,2,1,0:T(8,128)S(1)} %get-tuple-element.24), channel_id=1, source_target_pairs={{0,4},{4,8},{8,12},{12,16},{16,20},{20,24},{24,28},{1,5},{5,9},{9,... | collective-permute-start | bytes 393224 | tf_op jit(solution)/shard_map/ppermute | solution.py:21
  81.4 2.2 select_maximum_fusion.4
  87.6 5.9 %collective-permute-start.12 = (f32[32,1,8,128]{3,2,1,0:T(8,128)S(1)}, f32[32,1,8,128]{3,2,1,0:T(8,128)S(1)}, u32[]{:S(2)}, u32[]{:S(2)}) collective-permute-start(f32[32,1,8,128]{3,2,1,0:T(8,128)S(1)} %get-tuple-element.22), channel_id=1, source_target_pairs={{0,4},{4,8},{8,12},{12,16},{16,20},{20,24},{24,28},{1,5},{5,9},{9,... | collective-permute-start | bytes 393224 | tf_op jit(solution)/shard_map/ppermute | solution.py:21
  94.5 2.2 select_maximum_fusion.2
  100.8 6.6 %collective-permute-start.14 = (f32[32,1,8,128]{3,2,1,0:T(8,128)S(1)}, f32[32,1,8,128]{3,2,1,0:T(8,128)S(1)}, u32[]{:S(2)}, u32[]{:S(2)}) collective-permute-start(f32[32,1,8,128]{3,2,1,0:T(8,128)S(1)} %get-tuple-element.20), channel_id=1, source_target_pairs={{0,4},{4,8},{8,12},{12,16},{16,20},{20,24},{24,28},{1,5},{5,9},{9,... | collective-permute-start | bytes 393224 | tf_op jit(solution)/shard_map/ppermute | solution.py:21
  107.9 2.2 select_maximum_fusion
  113.8 1.6 copy.24
  115.5 93.3 %all-gather.3.cloned.1.call-done = f32[128,8192]{1,0:T(8,128)} async-done(((f32[32,8192]{1,0:T(8,128)}), f32[128,8192]{1,0:T(8,128)}) %all-gather.3.cloned.1.call-update) | async-done | bytes 4194320 | tf_op jit(solution)/shard_map/all_gather | solution.py:77
  208.7 7.6 %fusion.26 = f32[96,128]{0,1:T(8,128)S(1)} fusion(f32[128,8192]{1,0:T(8,128)} %all-gather.3.cloned.1.call-done, f32[12,8,64,128]{3,2,1,0:T(8,128)S(1)} %bitcast.36), kind=kOutput, calls=%fused_computation.95 | convolution fusion | flops 1207959552 | bytes 7389184 | tf_op jit(solution)/shard_map/dot_general | solution.py:79
  216.4 24.3 %psum.14 = f32[96,128]{0,1:T(8,128)S(1)} all-reduce(f32[96,128]{0,1:T(8,128)S(1)} %fusion.26), channel_id=1, replica_groups=mesh['slab'=8,'blk'=4] {'slab'}, use_global_device_ids=true, to_apply=%region_0.1 | all-reduce | flops 12288 | bytes 98304 | tf_op jit(solution)/shard_map/psum | solution.py:78
  240.7 7.9 %fusion.11 = f32[128,8192]{1,0:T(8,128)} fusion(f32[96,128]{0,1:T(8,128)S(1)} %psum.14, f32[12,8,64,128]{3,2,1,0:T(8,128)S(1)} %bitcast.37), kind=kOutput, calls=%fused_computation.56 | convolution fusion | flops 1207959552 | bytes 7389184 | tf_op jit(solution)/shard_map/dot_general | solution.py:88
  248.6 73.7 %reduce-scatter.2.cloned.1.call-done = f32[32,8192]{1,0:T(8,128)} async-done(((f32[128,8192]{1,0:T(8,128)}), f32[32,8192]{1,0:T(8,128)}) %reduce-scatter.2.cloned.1.call-update) | async-done | bytes 1048592 | tf_op jit(solution)/shard_map/reduce_scatter | solution.py:87
  322.4 2.8 fusion.147
  325.4 81.2 %all-gather.5.cloned.1.call-done = f32[128,8192]{1,0:T(8,128)} async-done(((f32[32,8192]{1,0:T(8,128)}), f32[128,8192]{1,0:T(8,128)}) %all-gather.5.cloned.1.call-update) | async-done | bytes 4194320 | tf_op jit(solution)/shard_map/all_gather | solution.py:98
  406.6 7.6 %fusion.163 = f32[128,128]{0,1:T(8,128)} fusion(f32[128,8192]{1,0:T(8,128)} %all-gather.5.cloned.1.call-done), kind=kOutput, calls=%fused_computation.283 | convolution fusion | flops 1610612736 | bytes 4259840 | tf_op jit(solution)/shard_map/dot_general | solution.py:100
  414.3 51.8 %all-reduce.10.cloned.1.call-done = f32[128,128]{0,1:T(8,128)} async-done(((f32[128,128]{0,1:T(8,128)}), f32[128,128]{0,1:T(8,128)}) %all-reduce.10.cloned.1.call-update) | async-done | bytes 65552 | tf_op jit(solution)/shard_map/psum | solution.py:99
  467.9 11.7 %cholesky.17 = f32[128,128]{1,0:T(8,128)S(1)} custom-call(f32[128,128]{1,0:T(8,128)S(1)} %fusion.142), custom_call_target="Cholesky" | custom-call | tf_op jit(solution)/shard_map/jit(cholesky)/cholesky | solution.py:50
  480.9 9.8 %custom-call.7 = f32[1,128,128]{1,2,0:T(8,128)S(1)} custom-call(f32[1,128,128]{2,1,0:T(8,128)S(1)} %fusion.139), custom_call_target="InvertDiagBlocksLowerTriangular" | custom-call | tf_op jit(solution)/shard_map/jit(_solve_triangular)/triangular_solve | solution.py:52
  491.0 4.0 fusion.25
  (81 shorter events, 43.9 us)
Async XLA Ops:
  6.5 202.2 %all-gather.3.cloned.1.call-start = ((), (), s32[]{:S(2)}) async-start(), calls=%async_computation.1 | async-start | bytes 5242880 | tf_op jit(solution)/shard_map/all_gather | solution.py:77
  9.5 5.1 %collective-permute-start.1 = (f32[32,1,8,128]{3,2,1,0:T(8,128)S(1)}, f32[32,1,8,128]{3,2,1,0:T(8,128)S(1)}, u32[]{:S(2)}, u32[]{:S(2)}) collective-permute-start(f32[32,1,8,128]{3,2,1,0:T(8,128)S(1)} %get-tuple-element.33), channel_id=1, source_target_pairs={{4,0},{8,4},{12,8},{16,12},{20,16},{24,20},{28,24},{5,1},{9,5},{13... | collective-permute-start | bytes 393224 | tf_op jit(solution)/shard_map/ppermute | solution.py:23
  10.8 4.0 collective-permute-start
  18.0 1.2 copy-start.1
  20.3 7.4 %collective-permute-start.3 = (f32[32,1,8,128]{3,2,1,0:T(8,128)S(1)}, f32[32,1,8,128]{3,2,1,0:T(8,128)S(1)}, u32[]{:S(2)}, u32[]{:S(2)}) collective-permute-start(f32[32,1,8,128]{3,2,1,0:T(8,128)S(1)} %get-tuple-element.31), channel_id=1, source_target_pairs={{4,0},{8,4},{12,8},{16,12},{20,16},{24,20},{28,24},{5,1},{9,5},{13... | collective-permute-start | bytes 393224 | tf_op jit(solution)/shard_map/ppermute | solution.py:23
  21.6 7.1 %collective-permute-start.2 = (f32[32,1,8,128]{3,2,1,0:T(8,128)S(1)}, f32[32,1,8,128]{3,2,1,0:T(8,128)S(1)}, u32[]{:S(2)}, u32[]{:S(2)}) collective-permute-start(f32[32,1,8,128]{3,2,1,0:T(8,128)S(1)} %get-tuple-element.32), channel_id=1, source_target_pairs={{0,4},{4,8},{8,12},{12,16},{16,20},{20,24},{24,28},{1,5},{5,9},{9,... | collective-permute-start | bytes 393224 | tf_op jit(solution)/shard_map/ppermute | solution.py:21
  33.6 7.4 %collective-permute-start.5 = (f32[32,1,8,128]{3,2,1,0:T(8,128)S(1)}, f32[32,1,8,128]{3,2,1,0:T(8,128)S(1)}, u32[]{:S(2)}, u32[]{:S(2)}) collective-permute-start(f32[32,1,8,128]{3,2,1,0:T(8,128)S(1)} %get-tuple-element.29), channel_id=1, source_target_pairs={{4,0},{8,4},{12,8},{16,12},{20,16},{24,20},{28,24},{5,1},{9,5},{13... | collective-permute-start | bytes 393224 | tf_op jit(solution)/shard_map/ppermute | solution.py:23
  34.9 6.9 %collective-permute-start.4 = (f32[32,1,8,128]{3,2,1,0:T(8,128)S(1)}, f32[32,1,8,128]{3,2,1,0:T(8,128)S(1)}, u32[]{:S(2)}, u32[]{:S(2)}) collective-permute-start(f32[32,1,8,128]{3,2,1,0:T(8,128)S(1)} %get-tuple-element.30), channel_id=1, source_target_pairs={{0,4},{4,8},{8,12},{12,16},{16,20},{20,24},{24,28},{1,5},{5,9},{9,... | collective-permute-start | bytes 393224 | tf_op jit(solution)/shard_map/ppermute | solution.py:21
  46.8 7.3 %collective-permute-start.7 = (f32[32,1,8,128]{3,2,1,0:T(8,128)S(1)}, f32[32,1,8,128]{3,2,1,0:T(8,128)S(1)}, u32[]{:S(2)}, u32[]{:S(2)}) collective-permute-start(f32[32,1,8,128]{3,2,1,0:T(8,128)S(1)} %get-tuple-element.27), channel_id=1, source_target_pairs={{4,0},{8,4},{12,8},{16,12},{20,16},{24,20},{28,24},{5,1},{9,5},{13... | collective-permute-start | bytes 393224 | tf_op jit(solution)/shard_map/ppermute | solution.py:23
  48.1 6.9 %collective-permute-start.6 = (f32[32,1,8,128]{3,2,1,0:T(8,128)S(1)}, f32[32,1,8,128]{3,2,1,0:T(8,128)S(1)}, u32[]{:S(2)}, u32[]{:S(2)}) collective-permute-start(f32[32,1,8,128]{3,2,1,0:T(8,128)S(1)} %get-tuple-element.28), channel_id=1, source_target_pairs={{0,4},{4,8},{8,12},{12,16},{16,20},{20,24},{24,28},{1,5},{5,9},{9,... | collective-permute-start | bytes 393224 | tf_op jit(solution)/shard_map/ppermute | solution.py:21
  60.0 7.3 %collective-permute-start.9 = (f32[32,1,8,128]{3,2,1,0:T(8,128)S(1)}, f32[32,1,8,128]{3,2,1,0:T(8,128)S(1)}, u32[]{:S(2)}, u32[]{:S(2)}) collective-permute-start(f32[32,1,8,128]{3,2,1,0:T(8,128)S(1)} %get-tuple-element.25), channel_id=1, source_target_pairs={{4,0},{8,4},{12,8},{16,12},{20,16},{24,20},{28,24},{5,1},{9,5},{13... | collective-permute-start | bytes 393224 | tf_op jit(solution)/shard_map/ppermute | solution.py:23
  61.3 6.9 %collective-permute-start.8 = (f32[32,1,8,128]{3,2,1,0:T(8,128)S(1)}, f32[32,1,8,128]{3,2,1,0:T(8,128)S(1)}, u32[]{:S(2)}, u32[]{:S(2)}) collective-permute-start(f32[32,1,8,128]{3,2,1,0:T(8,128)S(1)} %get-tuple-element.26), channel_id=1, source_target_pairs={{0,4},{4,8},{8,12},{12,16},{16,20},{20,24},{24,28},{1,5},{5,9},{9,... | collective-permute-start | bytes 393224 | tf_op jit(solution)/shard_map/ppermute | solution.py:21
  73.1 7.5 %collective-permute-start.11 = (f32[32,1,8,128]{3,2,1,0:T(8,128)S(1)}, f32[32,1,8,128]{3,2,1,0:T(8,128)S(1)}, u32[]{:S(2)}, u32[]{:S(2)}) collective-permute-start(f32[32,1,8,128]{3,2,1,0:T(8,128)S(1)} %get-tuple-element.23), channel_id=1, source_target_pairs={{4,0},{8,4},{12,8},{16,12},{20,16},{24,20},{28,24},{5,1},{9,5},{13... | collective-permute-start | bytes 393224 | tf_op jit(solution)/shard_map/ppermute | solution.py:23
  74.4 6.9 %collective-permute-start.10 = (f32[32,1,8,128]{3,2,1,0:T(8,128)S(1)}, f32[32,1,8,128]{3,2,1,0:T(8,128)S(1)}, u32[]{:S(2)}, u32[]{:S(2)}) collective-permute-start(f32[32,1,8,128]{3,2,1,0:T(8,128)S(1)} %get-tuple-element.24), channel_id=1, source_target_pairs={{0,4},{4,8},{8,12},{12,16},{16,20},{20,24},{24,28},{1,5},{5,9},{9,... | collective-permute-start | bytes 393224 | tf_op jit(solution)/shard_map/ppermute | solution.py:21
  86.3 7.3 %collective-permute-start.13 = (f32[32,1,8,128]{3,2,1,0:T(8,128)S(1)}, f32[32,1,8,128]{3,2,1,0:T(8,128)S(1)}, u32[]{:S(2)}, u32[]{:S(2)}) collective-permute-start(f32[32,1,8,128]{3,2,1,0:T(8,128)S(1)} %get-tuple-element.21), channel_id=1, source_target_pairs={{4,0},{8,4},{12,8},{16,12},{20,16},{24,20},{28,24},{5,1},{9,5},{13... | collective-permute-start | bytes 393224 | tf_op jit(solution)/shard_map/ppermute | solution.py:23
  87.6 6.9 %collective-permute-start.12 = (f32[32,1,8,128]{3,2,1,0:T(8,128)S(1)}, f32[32,1,8,128]{3,2,1,0:T(8,128)S(1)}, u32[]{:S(2)}, u32[]{:S(2)}) collective-permute-start(f32[32,1,8,128]{3,2,1,0:T(8,128)S(1)} %get-tuple-element.22), channel_id=1, source_target_pairs={{0,4},{4,8},{8,12},{12,16},{16,20},{20,24},{24,28},{1,5},{5,9},{9,... | collective-permute-start | bytes 393224 | tf_op jit(solution)/shard_map/ppermute | solution.py:21
  99.5 7.9 %collective-permute-start.15 = (f32[32,1,8,128]{3,2,1,0:T(8,128)S(1)}, f32[32,1,8,128]{3,2,1,0:T(8,128)S(1)}, u32[]{:S(2)}, u32[]{:S(2)}) collective-permute-start(f32[32,1,8,128]{3,2,1,0:T(8,128)S(1)} %get-tuple-element.19), channel_id=1, source_target_pairs={{4,0},{8,4},{12,8},{16,12},{20,16},{24,20},{28,24},{5,1},{9,5},{13... | collective-permute-start | bytes 393224 | tf_op jit(solution)/shard_map/ppermute | solution.py:23
  100.8 7.1 %collective-permute-start.14 = (f32[32,1,8,128]{3,2,1,0:T(8,128)S(1)}, f32[32,1,8,128]{3,2,1,0:T(8,128)S(1)}, u32[]{:S(2)}, u32[]{:S(2)}) collective-permute-start(f32[32,1,8,128]{3,2,1,0:T(8,128)S(1)} %get-tuple-element.20), channel_id=1, source_target_pairs={{0,4},{4,8},{8,12},{12,16},{16,20},{20,24},{24,28},{1,5},{5,9},{9,... | collective-permute-start | bytes 393224 | tf_op jit(solution)/shard_map/ppermute | solution.py:21
  111.7 97.0 %copy-start = (f32[96,8,8,128]{3,2,1,0:T(8,128)S(1)}, f32[96,8,8,128]{3,2,1,0:T(8,128)}, u32[]{:S(2)}) copy-start(f32[96,8,8,128]{3,2,1,0:T(8,128)} %param.5) | copy-start | bytes 9437188
  112.8 1.0 copy-start.2
  115.4 206.9 %reduce-scatter.2.cloned.1.call-start = ((), (), s32[]{:S(2)}) async-start(), calls=%async_computation.2 | async-start | bytes 5242880 | tf_op jit(solution)/shard_map/reduce_scatter | solution.py:87
  248.5 73.8 %copy-start.3 = (f32[32,8,8,128]{3,2,1,0:T(8,128)S(1)}, f32[32,8,8,128]{3,2,1,0:T(8,128)}, u32[]{:S(2)}) copy-start(f32[32,8,8,128]{3,2,1,0:T(8,128)} %copy-done.2) | copy-start | bytes 3145732
  248.6 158.1 %all-gather.5.cloned.1.call-start = ((), (), s32[]{:S(2)}) async-start(), calls=%async_computation.3 | async-start | bytes 5242880 | tf_op jit(solution)/shard_map/all_gather | solution.py:98
  325.2 140.9 %all-reduce.10.cloned.1.call-start = ((), (), s32[]{:S(2)}) async-start(), calls=%async_computation.4 | async-start | bytes 131072 | tf_op jit(solution)/shard_map/psum | solution.py:99
Sparse Core Ops, SparseCore 0:
  115.5 93.1 all-gather.2
  248.7 73.6 reduce-scatter.1
  325.3 81.2 all-gather.4
  414.4 51.6 all-reduce.9
where the time goes:
time: 510 us; the launch traced here: 503 us
  waiting for transfers between devices  306 us (60%)
  other arithmetic  69.2 us (14%)
  starting transfers between devices  56.4 us (11%)
  matrix products  27.3 us (5%)
  blocking collectives  24.3 us (5%)
  between operations  13.9 us (3%)
  local copies, waits for them, and re-layouts  5.53 us (1%)
    all_gather x1, waiting for transfers between devices, per_device(): gathered = lax.all_gather(flat, 'blk', axis=0, tiled=True)  93.3 us
    all_gather x1, waiting for transfers between devices, per_device(): deflated = lax.all_gather(own_deflated, 'blk', axis=0, tiled=True)  81.2 us
    reduce_scatter x1, waiting for transfers between devices, per_device(): lax.psum_scatter(jnp.dot(correlations.T, modes_flat, precision=lax.Precis...  73.7 us
    psum x1, waiting for transfers between devices, per_device(): lax.psum(jnp.dot(deflated, deflated.T, precision=lax.Precision.HIGHEST, p...  51.8 us
    ppermute x8, starting transfers between devices, padded_2(): lax.ppermute(tail, axis, [(i, (i + 1) % count) for i in range(ends)])  45.8 us
    psum x1, blocking collectives, per_device(): lax.psum(jnp.dot(modes_flat, gathered.T, precision=lax.Precision.HIGHEST,...  24.3 us
    concatenate x8, other arithmetic, padded_2(): jnp.concatenate([lax.ppermute(tail, axis, [(i, (i + 1) % count) for i in...  18 us
    another operation x3, other arithmetic, lower_inverse(): lower_factor = jnp.linalg.cholesky(gram)  12.4 us
  transfers between devices with their start and end apart: 20, of which 12 were waited for; matrix products, arithmetic and copies ran while one was open for 0% of the time, Pallas kernels for 0%

commit v1 on v0

--- a/solution.py
+++ b/solution.py
@@ -1,3 +1,4 @@
+import functools
 import jax
 import jax.numpy as jnp
 from jax import lax
@@ -8,6 +9,13 @@
 VOID_ROOT = 0.31622776601683794
 FILTER_CENTRE = 9.0
 FILTER_HALF = 7.5
+
+
+def run_trails_here(matrix, row_axis):
+    return lax.all_gather(matrix, axis_name=row_axis).sum(axis=0)
+
+
+meet_kinds_in = functools.partial(run_trails_here, row_axis="slab")
 
 
 def padded_2(cells, sides, width):
@@ -96,14 +104,13 @@
         tiled=True,
     )
     deflated = lax.all_gather(own_deflated, "blk", axis=0, tiled=True)
-    gram = lax.psum(
+    gram = meet_kinds_in(
         jnp.dot(
             deflated,
             deflated.T,
             precision=lax.Precision.HIGHEST,
             preferred_element_type=jnp.float32,
-        ),
-        "slab",
+        )
     )
     inverse = lower_inverse(gram)
     own_rows = lax.dynamic_slice_in_dim(inverse, lax.axis_index("blk") * own_count, own_count, 0)

time: 510 us -> 465 us (0.912)
  waiting for transfers between devices: 306 us -> 254 us
  blocking collectives: 24.3 us -> 34.1 us
    psum x1 -> x0, waiting for transfers between devices: 51.8 us -> none  [per_device(): lax.psum(jnp.dot(deflated, deflated.T, precision=lax.Precision.HIGHEST, p...]
    all_gather x0 -> x1, blocking collectives: none -> 9.81 us  [run_trails_here(): return lax.all_gather(matrix, axis_name=row_axis).sum(axis=0)]
  transfers between devices with their start and end apart: 20 -> 19, of which waited for: 12 -> 11; matrix products, arithmetic and copies ran while one was open for 0% -> 0% of each run, Pallas kernels for 0% -> 0%
where the time goes in v1:
time: 465 us; the launch traced here: 458 us
  waiting for transfers between devices  254 us (55%)
  other arithmetic  68.4 us (15%)
  starting transfers between devices  56.4 us (12%)
  blocking collectives  34.1 us (7%)
  matrix products  26.7 us (6%)
  between operations  13.9 us (3%)
  local copies, waits for them, and re-layouts  4.67 us (1%)
    all_gather x1, waiting for transfers between devices, per_device(): gathered = lax.all_gather(flat, 'blk', axis=0, tiled=True)  93.3 us
    all_gather x1, waiting for transfers between devices, per_device(): deflated = lax.all_gather(own_deflated, 'blk', axis=0, tiled=True)  81.4 us
    reduce_scatter x1, waiting for transfers between devices, per_device(): lax.psum_scatter(jnp.dot(correlations.T, modes_flat, precision=lax.Precis...  73.6 us
    ppermute x8, starting transfers between devices, padded_2(): lax.ppermute(tail, axis, [(i, (i + 1) % count) for i in range(ends)])  45.8 us
    psum x1, blocking collectives, per_device(): lax.psum(jnp.dot(modes_flat, gathered.T, precision=lax.Precision.HIGHEST,...  24.3 us
    concatenate x8, other arithmetic, padded_2(): jnp.concatenate([lax.ppermute(tail, axis, [(i, (i + 1) % count) for i in...  18 us
    another operation x3, other arithmetic, lower_inverse(): lower_factor = jnp.linalg.cholesky(gram)  12.4 us
    another operation x2, other arithmetic, lower_inverse(): return jax.scipy.linalg.solve_triangular(lower_factor, identity, lower=True)  10.5 us
  transfers between devices with their start and end apart: 19, of which 11 were waited for; matrix products, arithmetic and copies ran while one was open for 0% of the time, Pallas kernels for 0%

profile of v1, /device:TPU:0, one launch (start us, length us, event | category | flops | bytes accessed | tf_op | source)
XLA Modules:
  0.0 458.5 jit_solution(6563126949798105353)
XLA Ops:
  8.1 1.4 multiply_multiply_fusion.7
  9.5 1.3 collective-permute-start.1
  10.8 3.0 collective-permute-start
  14.8 2.2 select_maximum_fusion.14
  21.6 6.1 %collective-permute-start.2 = (f32[32,1,8,128]{3,2,1,0:T(8,128)S(1)}, f32[32,1,8,128]{3,2,1,0:T(8,128)S(1)}, u32[]{:S(2)}, u32[]{:S(2)}) collective-permute-start(f32[32,1,8,128]{3,2,1,0:T(8,128)S(1)} %get-tuple-element.32), channel_id=1, source_target_pairs={{0,4},{4,8},{8,12},{12,16},{16,20},{20,24},{24,28},{1,5},{5,9},{9,... | collective-permute-start | bytes 393224 | tf_op jit(solution)/shard_map/ppermute | solution.py:29
  28.7 2.2 select_maximum_fusion.12
  34.9 6.1 %collective-permute-start.4 = (f32[32,1,8,128]{3,2,1,0:T(8,128)S(1)}, f32[32,1,8,128]{3,2,1,0:T(8,128)S(1)}, u32[]{:S(2)}, u32[]{:S(2)}) collective-permute-start(f32[32,1,8,128]{3,2,1,0:T(8,128)S(1)} %get-tuple-element.30), channel_id=1, source_target_pairs={{0,4},{4,8},{8,12},{12,16},{16,20},{20,24},{24,28},{1,5},{5,9},{9,... | collective-permute-start | bytes 393224 | tf_op jit(solution)/shard_map/ppermute | solution.py:29
  41.8 2.2 select_maximum_fusion.10
  46.8 1.3 collective-permute-start.7
  48.1 5.9 %collective-permute-start.6 = (f32[32,1,8,128]{3,2,1,0:T(8,128)S(1)}, f32[32,1,8,128]{3,2,1,0:T(8,128)S(1)}, u32[]{:S(2)}, u32[]{:S(2)}) collective-permute-start(f32[32,1,8,128]{3,2,1,0:T(8,128)S(1)} %get-tuple-element.28), channel_id=1, source_target_pairs={{0,4},{4,8},{8,12},{12,16},{16,20},{20,24},{24,28},{1,5},{5,9},{9,... | collective-permute-start | bytes 393224 | tf_op jit(solution)/shard_map/ppermute | solution.py:29
  55.0 2.2 select_maximum_fusion.8
  61.3 5.9 %collective-permute-start.8 = (f32[32,1,8,128]{3,2,1,0:T(8,128)S(1)}, f32[32,1,8,128]{3,2,1,0:T(8,128)S(1)}, u32[]{:S(2)}, u32[]{:S(2)}) collective-permute-start(f32[32,1,8,128]{3,2,1,0:T(8,128)S(1)} %get-tuple-element.26), channel_id=1, source_target_pairs={{0,4},{4,8},{8,12},{12,16},{16,20},{20,24},{24,28},{1,5},{5,9},{9,... | collective-permute-start | bytes 393224 | tf_op jit(solution)/shard_map/ppermute | solution.py:29
  68.2 2.2 select_maximum_fusion.6
  74.4 6.2 %collective-permute-start.10 = (f32[32,1,8,128]{3,2,1,0:T(8,128)S(1)}, f32[32,1,8,128]{3,2,1,0:T(8,128)S(1)}, u32[]{:S(2)}, u32[]{:S(2)}) collective-permute-start(f32[32,1,8,128]{3,2,1,0:T(8,128)S(1)} %get-tuple-element.24), channel_id=1, source_target_pairs={{0,4},{4,8},{8,12},{12,16},{16,20},{20,24},{24,28},{1,5},{5,9},{9,... | collective-permute-start | bytes 393224 | tf_op jit(solution)/shard_map/ppermute | solution.py:29
  81.3 2.2 select_maximum_fusion.4
  87.6 5.9 %collective-permute-start.12 = (f32[32,1,8,128]{3,2,1,0:T(8,128)S(1)}, f32[32,1,8,128]{3,2,1,0:T(8,128)S(1)}, u32[]{:S(2)}, u32[]{:S(2)}) collective-permute-start(f32[32,1,8,128]{3,2,1,0:T(8,128)S(1)} %get-tuple-element.22), channel_id=1, source_target_pairs={{0,4},{4,8},{8,12},{12,16},{16,20},{20,24},{24,28},{1,5},{5,9},{9,... | collective-permute-start | bytes 393224 | tf_op jit(solution)/shard_map/ppermute | solution.py:29
  94.5 2.2 select_maximum_fusion.2
  100.7 6.6 %collective-permute-start.14 = (f32[32,1,8,128]{3,2,1,0:T(8,128)S(1)}, f32[32,1,8,128]{3,2,1,0:T(8,128)S(1)}, u32[]{:S(2)}, u32[]{:S(2)}) collective-permute-start(f32[32,1,8,128]{3,2,1,0:T(8,128)S(1)} %get-tuple-element.20), channel_id=1, source_target_pairs={{0,4},{4,8},{8,12},{12,16},{16,20},{20,24},{24,28},{1,5},{5,9},{9,... | collective-permute-start | bytes 393224 | tf_op jit(solution)/shard_map/ppermute | solution.py:29
  107.9 2.2 select_maximum_fusion
  113.8 1.6 copy.23
  115.4 93.3 %all-gather.4.cloned.1.call-done = f32[128,8192]{1,0:T(8,128)} async-done(((f32[32,8192]{1,0:T(8,128)}), f32[128,8192]{1,0:T(8,128)}) %all-gather.4.cloned.1.call-update) | async-done | bytes 4194320 | tf_op jit(solution)/shard_map/all_gather | solution.py:85
  208.7 7.6 %fusion.26 = f32[96,128]{0,1:T(8,128)S(1)} fusion(f32[128,8192]{1,0:T(8,128)} %all-gather.4.cloned.1.call-done, f32[12,8,64,128]{3,2,1,0:T(8,128)S(1)} %bitcast.37), kind=kOutput, calls=%fused_computation.95 | convolution fusion | flops 1207959552 | bytes 7389184 | tf_op jit(solution)/shard_map/dot_general | solution.py:87
  216.3 24.3 %psum.7 = f32[96,128]{0,1:T(8,128)S(1)} all-reduce(f32[96,128]{0,1:T(8,128)S(1)} %fusion.26), channel_id=1, replica_groups=mesh['slab'=8,'blk'=4] {'slab'}, use_global_device_ids=true, to_apply=%region_0.1 | all-reduce | flops 12288 | bytes 98304 | tf_op jit(solution)/shard_map/psum | solution.py:86
  240.6 7.8 %fusion.11 = f32[128,8192]{1,0:T(8,128)} fusion(f32[96,128]{0,1:T(8,128)S(1)} %psum.7, f32[12,8,64,128]{3,2,1,0:T(8,128)S(1)} %bitcast.38), kind=kOutput, calls=%fused_computation.56 | convolution fusion | flops 1207959552 | bytes 7389184 | tf_op jit(solution)/shard_map/dot_general | solution.py:96
  248.7 73.6 %reduce-scatter.2.cloned.1.call-done = f32[32,8192]{1,0:T(8,128)} async-done(((f32[128,8192]{1,0:T(8,128)}), f32[32,8192]{1,0:T(8,128)}) %reduce-scatter.2.cloned.1.call-update) | async-done | bytes 1048592 | tf_op jit(solution)/shard_map/reduce_scatter | solution.py:95
  322.3 2.8 fusion.147
  325.2 81.4 %all-gather.6.cloned.1.call-done = f32[128,8192]{1,0:T(8,128)} async-done(((f32[32,8192]{1,0:T(8,128)}), f32[128,8192]{1,0:T(8,128)}) %all-gather.6.cloned.1.call-update) | async-done | bytes 4194320 | tf_op jit(solution)/shard_map/all_gather | solution.py:106
  406.6 7.0 %fusion.163 = f32[128,128]{1,0:T(8,128)S(1)} fusion(f32[128,8192]{1,0:T(8,128)} %all-gather.6.cloned.1.call-done), kind=kOutput, calls=%fused_computation.283 | convolution fusion | flops 1610612736 | bytes 4259840 | tf_op jit(solution)/shard_map/dot_general | solution.py:108
  413.5 9.8 %all-gather = f32[1024,128]{1,0:T(8,128)S(1)} all-gather(f32[128,128]{1,0:T(8,128)S(1)} %fusion.163), channel_id=2, replica_groups=mesh['slab'=8,'blk'=4] {'slab'}, dimensions={0}, use_global_device_ids=true | all-gather | bytes 589824 | tf_op jit(solution)/shard_map/all_gather | solution.py:15
  423.5 11.7 %cholesky.17 = f32[128,128]{1,0:T(8,128)S(1)} custom-call(f32[128,128]{1,0:T(8,128)S(1)} %fusion.142), custom_call_target="Cholesky" | custom-call | tf_op jit(solution)/shard_map/jit(cholesky)/cholesky | solution.py:58
  436.5 9.8 %custom-call.7 = f32[1,128,128]{1,2,0:T(8,128)S(1)} custom-call(f32[1,128,128]{2,1,0:T(8,128)S(1)} %fusion.139), custom_call_target="InvertDiagBlocksLowerTriangular" | custom-call | tf_op jit(solution)/shard_map/jit(_solve_triangular)/triangular_solve | solution.py:60
  446.6 4.0 fusion.25
  (80 shorter events, 42.2 us)
Async XLA Ops:
  6.5 202.1 %all-gather.4.cloned.1.call-start = ((), (), s32[]{:S(2)}) async-start(), calls=%async_computation.1 | async-start | bytes 5242880 | tf_op jit(solution)/shard_map/all_gather | solution.py:85
  9.5 5.1 %collective-permute-start.1 = (f32[32,1,8,128]{3,2,1,0:T(8,128)S(1)}, f32[32,1,8,128]{3,2,1,0:T(8,128)S(1)}, u32[]{:S(2)}, u32[]{:S(2)}) collective-permute-start(f32[32,1,8,128]{3,2,1,0:T(8,128)S(1)} %get-tuple-element.33), channel_id=1, source_target_pairs={{4,0},{8,4},{12,8},{16,12},{20,16},{24,20},{28,24},{5,1},{9,5},{13... | collective-permute-start | bytes 393224 | tf_op jit(solution)/shard_map/ppermute | solution.py:31
  10.8 4.0 collective-permute-start
  18.0 1.2 copy-start.1
  20.3 7.4 %collective-permute-start.3 = (f32[32,1,8,128]{3,2,1,0:T(8,128)S(1)}, f32[32,1,8,128]{3,2,1,0:T(8,128)S(1)}, u32[]{:S(2)}, u32[]{:S(2)}) collective-permute-start(f32[32,1,8,128]{3,2,1,0:T(8,128)S(1)} %get-tuple-element.31), channel_id=1, source_target_pairs={{4,0},{8,4},{12,8},{16,12},{20,16},{24,20},{28,24},{5,1},{9,5},{13... | collective-permute-start | bytes 393224 | tf_op jit(solution)/shard_map/ppermute | solution.py:31
  21.6 7.1 %collective-permute-start.2 = (f32[32,1,8,128]{3,2,1,0:T(8,128)S(1)}, f32[32,1,8,128]{3,2,1,0:T(8,128)S(1)}, u32[]{:S(2)}, u32[]{:S(2)}) collective-permute-start(f32[32,1,8,128]{3,2,1,0:T(8,128)S(1)} %get-tuple-element.32), channel_id=1, source_target_pairs={{0,4},{4,8},{8,12},{12,16},{16,20},{20,24},{24,28},{1,5},{5,9},{9,... | collective-permute-start | bytes 393224 | tf_op jit(solution)/shard_map/ppermute | solution.py:29
  33.6 7.4 %collective-permute-start.5 = (f32[32,1,8,128]{3,2,1,0:T(8,128)S(1)}, f32[32,1,8,128]{3,2,1,0:T(8,128)S(1)}, u32[]{:S(2)}, u32[]{:S(2)}) collective-permute-start(f32[32,1,8,128]{3,2,1,0:T(8,128)S(1)} %get-tuple-element.29), channel_id=1, source_target_pairs={{4,0},{8,4},{12,8},{16,12},{20,16},{24,20},{28,24},{5,1},{9,5},{13... | collective-permute-start | bytes 393224 | tf_op jit(solution)/shard_map/ppermute | solution.py:31
  34.9 6.9 %collective-permute-start.4 = (f32[32,1,8,128]{3,2,1,0:T(8,128)S(1)}, f32[32,1,8,128]{3,2,1,0:T(8,128)S(1)}, u32[]{:S(2)}, u32[]{:S(2)}) collective-permute-start(f32[32,1,8,128]{3,2,1,0:T(8,128)S(1)} %get-tuple-element.30), channel_id=1, source_target_pairs={{0,4},{4,8},{8,12},{12,16},{16,20},{20,24},{24,28},{1,5},{5,9},{9,... | collective-permute-start | bytes 393224 | tf_op jit(solution)/shard_map/ppermute | solution.py:29
  46.8 7.3 %collective-permute-start.7 = (f32[32,1,8,128]{3,2,1,0:T(8,128)S(1)}, f32[32,1,8,128]{3,2,1,0:T(8,128)S(1)}, u32[]{:S(2)}, u32[]{:S(2)}) collective-permute-start(f32[32,1,8,128]{3,2,1,0:T(8,128)S(1)} %get-tuple-element.27), channel_id=1, source_target_pairs={{4,0},{8,4},{12,8},{16,12},{20,16},{24,20},{28,24},{5,1},{9,5},{13... | collective-permute-start | bytes 393224 | tf_op jit(solution)/shard_map/ppermute | solution.py:31
  48.1 6.9 %collective-permute-start.6 = (f32[32,1,8,128]{3,2,1,0:T(8,128)S(1)}, f32[32,1,8,128]{3,2,1,0:T(8,128)S(1)}, u32[]{:S(2)}, u32[]{:S(2)}) collective-permute-start(f32[32,1,8,128]{3,2,1,0:T(8,128)S(1)} %get-tuple-element.28), channel_id=1, source_target_pairs={{0,4},{4,8},{8,12},{12,16},{16,20},{20,24},{24,28},{1,5},{5,9},{9,... | collective-permute-start | bytes 393224 | tf_op jit(solution)/shard_map/ppermute | solution.py:29
  60.0 7.3 %collective-permute-start.9 = (f32[32,1,8,128]{3,2,1,0:T(8,128)S(1)}, f32[32,1,8,128]{3,2,1,0:T(8,128)S(1)}, u32[]{:S(2)}, u32[]{:S(2)}) collective-permute-start(f32[32,1,8,128]{3,2,1,0:T(8,128)S(1)} %get-tuple-element.25), channel_id=1, source_target_pairs={{4,0},{8,4},{12,8},{16,12},{20,16},{24,20},{28,24},{5,1},{9,5},{13... | collective-permute-start | bytes 393224 | tf_op jit(solution)/shard_map/ppermute | solution.py:31
  61.3 6.9 %collective-permute-start.8 = (f32[32,1,8,128]{3,2,1,0:T(8,128)S(1)}, f32[32,1,8,128]{3,2,1,0:T(8,128)S(1)}, u32[]{:S(2)}, u32[]{:S(2)}) collective-permute-start(f32[32,1,8,128]{3,2,1,0:T(8,128)S(1)} %get-tuple-element.26), channel_id=1, source_target_pairs={{0,4},{4,8},{8,12},{12,16},{16,20},{20,24},{24,28},{1,5},{5,9},{9,... | collective-permute-start | bytes 393224 | tf_op jit(solution)/shard_map/ppermute | solution.py:29
  73.1 7.5 %collective-permute-start.11 = (f32[32,1,8,128]{3,2,1,0:T(8,128)S(1)}, f32[32,1,8,128]{3,2,1,0:T(8,128)S(1)}, u32[]{:S(2)}, u32[]{:S(2)}) collective-permute-start(f32[32,1,8,128]{3,2,1,0:T(8,128)S(1)} %get-tuple-element.23), channel_id=1, source_target_pairs={{4,0},{8,4},{12,8},{16,12},{20,16},{24,20},{28,24},{5,1},{9,5},{13... | collective-permute-start | bytes 393224 | tf_op jit(solution)/shard_map/ppermute | solution.py:31
  74.4 6.9 %collective-permute-start.10 = (f32[32,1,8,128]{3,2,1,0:T(8,128)S(1)}, f32[32,1,8,128]{3,2,1,0:T(8,128)S(1)}, u32[]{:S(2)}, u32[]{:S(2)}) collective-permute-start(f32[32,1,8,128]{3,2,1,0:T(8,128)S(1)} %get-tuple-element.24), channel_id=1, source_target_pairs={{0,4},{4,8},{8,12},{12,16},{16,20},{20,24},{24,28},{1,5},{5,9},{9,... | collective-permute-start | bytes 393224 | tf_op jit(solution)/shard_map/ppermute | solution.py:29
  86.3 7.3 %collective-permute-start.13 = (f32[32,1,8,128]{3,2,1,0:T(8,128)S(1)}, f32[32,1,8,128]{3,2,1,0:T(8,128)S(1)}, u32[]{:S(2)}, u32[]{:S(2)}) collective-permute-start(f32[32,1,8,128]{3,2,1,0:T(8,128)S(1)} %get-tuple-element.21), channel_id=1, source_target_pairs={{4,0},{8,4},{12,8},{16,12},{20,16},{24,20},{28,24},{5,1},{9,5},{13... | collective-permute-start | bytes 393224 | tf_op jit(solution)/shard_map/ppermute | solution.py:31
  87.6 6.9 %collective-permute-start.12 = (f32[32,1,8,128]{3,2,1,0:T(8,128)S(1)}, f32[32,1,8,128]{3,2,1,0:T(8,128)S(1)}, u32[]{:S(2)}, u32[]{:S(2)}) collective-permute-start(f32[32,1,8,128]{3,2,1,0:T(8,128)S(1)} %get-tuple-element.22), channel_id=1, source_target_pairs={{0,4},{4,8},{8,12},{12,16},{16,20},{20,24},{24,28},{1,5},{5,9},{9,... | collective-permute-start | bytes 393224 | tf_op jit(solution)/shard_map/ppermute | solution.py:29
  99.4 7.9 %collective-permute-start.15 = (f32[32,1,8,128]{3,2,1,0:T(8,128)S(1)}, f32[32,1,8,128]{3,2,1,0:T(8,128)S(1)}, u32[]{:S(2)}, u32[]{:S(2)}) collective-permute-start(f32[32,1,8,128]{3,2,1,0:T(8,128)S(1)} %get-tuple-element.19), channel_id=1, source_target_pairs={{4,0},{8,4},{12,8},{16,12},{20,16},{24,20},{28,24},{5,1},{9,5},{13... | collective-permute-start | bytes 393224 | tf_op jit(solution)/shard_map/ppermute | solution.py:31
  100.7 7.1 %collective-permute-start.14 = (f32[32,1,8,128]{3,2,1,0:T(8,128)S(1)}, f32[32,1,8,128]{3,2,1,0:T(8,128)S(1)}, u32[]{:S(2)}, u32[]{:S(2)}) collective-permute-start(f32[32,1,8,128]{3,2,1,0:T(8,128)S(1)} %get-tuple-element.20), channel_id=1, source_target_pairs={{0,4},{4,8},{8,12},{12,16},{16,20},{20,24},{24,28},{1,5},{5,9},{9,... | collective-permute-start | bytes 393224 | tf_op jit(solution)/shard_map/ppermute | solution.py:29
  111.7 97.0 %copy-start = (f32[96,8,8,128]{3,2,1,0:T(8,128)S(1)}, f32[96,8,8,128]{3,2,1,0:T(8,128)}, u32[]{:S(2)}) copy-start(f32[96,8,8,128]{3,2,1,0:T(8,128)} %param.5) | copy-start | bytes 9437188
  112.8 1.0 copy-start.2
  115.4 206.9 %reduce-scatter.2.cloned.1.call-start = ((), (), s32[]{:S(2)}) async-start(), calls=%async_computation.2 | async-start | bytes 5242880 | tf_op jit(solution)/shard_map/reduce_scatter | solution.py:95
  248.5 73.8 %copy-start.3 = (f32[32,8,8,128]{3,2,1,0:T(8,128)S(1)}, f32[32,8,8,128]{3,2,1,0:T(8,128)}, u32[]{:S(2)}) copy-start(f32[32,8,8,128]{3,2,1,0:T(8,128)} %copy-done.2) | copy-start | bytes 3145732
  248.5 158.1 %all-gather.6.cloned.1.call-start = ((), (), s32[]{:S(2)}) async-start(), calls=%async_computation.3 | async-start | bytes 5242880 | tf_op jit(solution)/shard_map/all_gather | solution.py:106
Sparse Core Ops, SparseCore 0:
  115.5 93.1 all-gather.3
  248.6 73.6 reduce-scatter.1
  325.3 81.2 all-gather.5
